TPU v7x, 256 devices: a whole 4x4x8 slice. The times are simulated.
256 devices in a mesh: seq: 16 (over z, core), head: 16 (over x, y).
Axes of the slice: x: 4, y: 4, z: 8, core: 2. Of those that a mesh axis runs over, the one named last changes fastest.
Arguments:
- features: bfloat16 [65536, 8192], P(('seq', 'head')), may hold values from -6 to 6
- step_size: float32 [65536, 128], P(('seq', 'head')), may hold values from 0.01 to 0.08
- log_decay: float32 [65536, 128], P(('seq', 'head')), may hold values from -0.6 to 0
- inject: bfloat16 [65536, 1024], P(('seq', 'head')), may hold values from -1.5 to 1.5
- readout: bfloat16 [65536, 1024], P(('seq', 'head')), may hold values from -1.5 to 1.5
- skip_gain: float32 [128], replicated, may hold values from 0.5 to 1.5
Outputs:
- mixer_out: bfloat16 [65536, 8192], P(('seq', 'head'))
All inputs are finite; a program needn't handle non-finite values.
Results may differ from a plain program's by a relative error of at most 0.02.
Values may be sent and summed in bfloat16 or wider, within the bound.
No kernel may reach another device: no remote copies, remote signals or barrier semaphores. Data moves between devices by JAX's collectives and lax.ppermute only.
A program may use at most 128 MiB of HBM per device.

v0:
```python
import jax
import jax.numpy as jnp
from jax import lax
from jax.sharding import PartitionSpec as P

HEAD_DIM = 64
STATE = 128
GROUPS = 8
SPAN = 512


def entering_2(x, axis, join, neutral):
    place = lax.axis_index(axis)
    gathered = jax.tree.map(
        lambda a, kind: lax.all_gather(a.astype(kind), axis), x, (jnp.bfloat16, jnp.bfloat16)
    )
    state = jax.tree.map(lambda a, e: jnp.zeros_like(a) + jnp.asarray(e, a.dtype), x, neutral)

    def one(step, state):
        return join(
            state,
            jax.tree.map(
                lambda a, own: lax.dynamic_index_in_dim(a, step, 0, False).astype(own.dtype),
                gathered,
                x,
            ),
        )

    return lax.fori_loop(0, place, one, state)


def shards(features, step_size, log_decay, inject, readout, skip_gain):
    head_ways = lax.axis_size("head")
    head_index = lax.axis_index("head")
    heads_all = step_size.shape[1]
    local_heads = heads_all // head_ways
    group_heads = heads_all // GROUPS
    local_groups = max(1, local_heads // group_heads)
    per_group = local_heads // local_groups
    regrouped = lax.all_to_all(features, "head", split_axis=1, concat_axis=0, tiled=True)
    steps_local, decay_local = (
        lax.all_to_all(
            step_size.astype(jnp.bfloat16), "head", split_axis=1, concat_axis=0, tiled=True
        ).astype(step_size.dtype),
        lax.all_to_all(
            log_decay.astype(jnp.bfloat16), "head", split_axis=1, concat_axis=0, tiled=True
        ).astype(log_decay.dtype),
    )
    inject_all, readout_all = (
        lax.all_gather(inject, "head", axis=0, tiled=True),
        lax.all_gather(readout, "head", axis=0, tiled=True),
    )
    first_col = head_index * local_heads // group_heads * STATE
    inject_mine = lax.dynamic_slice_in_dim(inject_all, first_col, local_groups * STATE, 1)
    readout_mine = lax.dynamic_slice_in_dim(readout_all, first_col, local_groups * STATE, 1)
    seq_rows = regrouped.shape[0]
    spans = seq_rows // SPAN
    drive = (
        regrouped.reshape(seq_rows, local_heads, HEAD_DIM).astype(jnp.float32)
        * steps_local[:, :, None]
    ).astype(jnp.bfloat16)
    drive_q = drive.reshape(spans, SPAN, local_groups, per_group, HEAD_DIM)
    cum_q = jnp.cumsum(decay_local.reshape(spans, SPAN, local_heads), axis=1)
    inject_q = inject_mine.reshape(spans, SPAN, local_groups, STATE)
    readout_q = readout_mine.reshape(spans, SPAN, local_groups, STATE)
    row_ids = lax.broadcasted_iota(jnp.int32, (SPAN, SPAN), 0)
    col_ids = lax.broadcasted_iota(jnp.int32, (SPAN, SPAN), 1)
    lower_mask = row_ids >= col_ids

    def span_terms(pieces):
        read_c, inject_c, drive_c, cum_c = pieces
        intersection = jnp.einsum(
            "ign,jgn->gij", read_c, inject_c, preferred_element_type=jnp.float32
        )
        cum_heads = cum_c.T
        log_gap = cum_heads[:, :, None] - cum_heads[:, None, :]
        decays = jnp.where(lower_mask, jnp.exp(jnp.where(lower_mask, log_gap, 0.0)), 0.0)
        weights = (
            decays.reshape(local_groups, per_group, SPAN, SPAN) * intersection[:, None]
        ).astype(jnp.bfloat16)
        inner_out = jnp.einsum(
            "ghij,jghp->ighp", weights, drive_c, preferred_element_type=jnp.float32
        )
        tail_decay = jnp.exp(cum_heads[:, -1:] - cum_heads)
        scaled = (
            drive_c.astype(jnp.float32)
            * tail_decay.T.reshape(SPAN, local_groups, per_group)[..., None]
        ).astype(jnp.bfloat16)
        summary = jnp.einsum("jghp,jgn->ghpn", scaled, inject_c, preferred_element_type=jnp.float32)
        return (inner_out, summary.reshape(local_heads, HEAD_DIM, STATE))

    inner_out, summary = lax.map(span_terms, (readout_q, inject_q, drive_q, cum_q))
    totals = cum_q[:, -1, :]

    def advance(carried, pieces):
        block_total, summary_c = pieces
        updated = carried * jnp.exp(block_total)[:, None, None] + summary_c
        return (updated, carried)

    zero_state = jnp.zeros((local_heads, HEAD_DIM, STATE), jnp.float32)
    end_state, entering = lax.scan(advance, zero_state, (totals, summary))
    dev_total = jnp.sum(totals, axis=0)

    def combine(earlier, following):
        return (
            earlier[0] + following[0],
            earlier[1] * jnp.exp(following[0])[:, None, None] + following[1],
        )

    identity = (jnp.zeros((local_heads,), jnp.float32), zero_state)
    scanned = entering_2((dev_total, end_state), "seq", combine, identity)
    incoming = scanned[1]
    before = jnp.cumsum(totals, axis=0) - totals
    states = entering + jnp.exp(before)[:, :, None, None] * incoming[None]
    held = states.astype(jnp.bfloat16).reshape(spans, local_groups, per_group, HEAD_DIM, STATE)
    outer_out = jnp.einsum("cign,cghpn->cighp", readout_q, held, preferred_element_type=jnp.float32)
    outer_out = outer_out * jnp.exp(cum_q).reshape(spans, SPAN, local_groups, per_group)[..., None]
    skip_local = lax.dynamic_slice_in_dim(skip_gain, head_index * local_heads, local_heads)
    plain = regrouped.reshape(spans, SPAN, local_groups, per_group, HEAD_DIM).astype(jnp.float32)
    total_out = (
        inner_out + outer_out + skip_local.reshape(local_groups, per_group)[:, :, None] * plain
    )
    mixed_rows = total_out.astype(jnp.bfloat16).reshape(seq_rows, local_heads * HEAD_DIM)
    return lax.all_to_all(mixed_rows, "head", split_axis=0, concat_axis=1, tiled=True)


def solution(mesh):
    placed = (
        P(("seq", "head"), None),
        P(("seq", "head"), None),
        P(("seq", "head"), None),
        P(("seq", "head"), None),
        P(("seq", "head"), None),
        P(),
    )
    return jax.shard_map(
        shards, mesh=mesh, in_specs=placed, out_specs=P(("seq", "head"), None), check_vma=False
    )
```

profile of v0, /device:TPU:225, one launch (start us, length us, event | category | flops | bytes accessed | tf_op | source)
XLA Modules:
  0.0 422.0 jit_solution(15952692852257553255)
XLA Ops:
  9.6 6.8 %all-to-all-start.2 = ((bf16[256,16,8]{0,2,1:T(8,128)(2,1)}), bf16[256,16,8]{0,2,1:T(8,128)(2,1)S(1)}, u32[]{:S(2)}, u32[]{:S(2)}) async-start(bf16[256,16,8]{0,2,1:T(8,128)(2,1)} %bitcast.102), calls=%async_computation.2 | async-start | bytes 131072 | tf_op jit(solution)/shard_map/all_to_all | solution.py:45
  18.0 4.9 %all-to-all-done.2 = bf16[256,16,8]{0,2,1:T(8,128)(2,1)S(1)} async-done(((bf16[256,16,8]{0,2,1:T(8,128)(2,1)}), bf16[256,16,8]{0,2,1:T(8,128)(2,1)S(1)}, u32[]{:S(2)}, u32[]{:S(2)}) %all-to-all-start.2) | async-done | bytes 65568 | tf_op jit(solution)/shard_map/all_to_all | solution.py:45
  22.9 3.5 all-to-all-start.1
  26.4 6.4 %copy.78 = bf16[256,8192]{0,1:T(8,128)(2,1)} copy(bf16[256,8192]{1,0:T(8,128)(2,1)} %param.12) | data formatting | bytes 8388608 | tf_op args[0]
  33.2 6.3 %all-to-all-start = ((bf16[256,16,512]{0,2,1:T(8,128)(2,1)}), bf16[256,16,512]{0,2,1:T(8,128)(2,1)}, u32[]{:S(2)}, u32[]{:S(2)}) async-start(bf16[256,16,512]{0,2,1:T(8,128)(2,1)} %bitcast.134), calls=%async_computation | async-start | bytes 8388608 | tf_op jit(solution)/shard_map/all_to_all | solution.py:40
  39.6 9.0 %reduce-window.6 = f32[8,8,4,128]{3,1,2,0:T(8,128)S(1)} reduce-window(f32[8,8,4,128]{3,1,2,0:T(8,128)S(1)} %bitcast.139, f32[]{:T(128)} %constant.75.clone.1), window={size=1x1x1x128 pad=0_0x0_0x0_0x127_0}, to_apply=%region_0.1 | reduce-window | flops 4161536 | bytes 262148 | tf_op jit(solution)/shard_map/reduce-window
  49.6 65.2 %all-to-all-done = bf16[256,16,512]{0,2,1:T(8,128)(2,1)} async-done(((bf16[256,16,512]{0,2,1:T(8,128)(2,1)}), bf16[256,16,512]{0,2,1:T(8,128)(2,1)}, u32[]{:S(2)}, u32[]{:S(2)}) %all-to-all-start) | async-done | bytes 4194336 | tf_op jit(solution)/shard_map/all_to_all | solution.py:40
  114.8 3.1 convert_bitcast_fusion
  117.9 8.1 %copy.79 = f32[16,256,512]{1,0,2:T(8,128)} copy(f32[16,256,512]{1,2,0:T(8,128)S(1)} %convert_bitcast_fusion) | data formatting | bytes 16777216 | tf_op jit(solution)/shard_map/convert_element_type | solution.py:59
  125.9 9.8 %reshape.178 = f32[8,512,1,8,64]{1,0,4,3,2:T(8,128)} reshape(f32[16,256,512]{1,0,2:T(8,128)} %copy.79) | data formatting | bytes 16777216 | tf_op jit(solution)/shard_map/convert_element_type | solution.py:59
  135.7 5.1 %multiply_convert_fusion.7 = bf16[8,512,1,8,64]{1,0,4,3,2:T(8,128)(2,1)S(1)} fusion(f32[8,512,1,8,64]{1,0,4,3,2:T(8,128)} %reshape.178, f32[8,512,8]{1,0,2:T(8,128)S(1)} %copy.81), kind=kLoop, calls=%fused_computation.43 | loop fusion | flops 4194304 | bytes 12713984 | tf_op jit(solution)/shard_map/convert_element_type | solution.py:61
  140.8 3.5 copy.85
  145.6 54.1 %all-gather.8.cloned.1.call-done = bf16[4096,1024]{1,0:T(8,128)(2,1)} async-done(((bf16[256,1024]{1,0:T(8,128)(2,1)}), bf16[4096,1024]{1,0:T(8,128)(2,1)}) %all-gather.8.cloned.1.call-update) | async-done | bytes 8388624 | tf_op jit(solution)/shard_map/all_gather | solution.py:50
  202.6 59.0 %while.40 = (s32[]{:T(128)}, f32[8,512,1,8,64]{1,4,3,2,0:T(8,128)}, f32[8,8,64,128]{3,2,1,0:T(8,128)}, bf16[8,512,1,8,64]{1,4,3,2,0:T(8,128)(2,1)}, f32[8,512,8]...) while((s32[]{:T(128)}, f32[8,512,1,8,64]{1,4,3,2,0:T(8,128)}, ...), condition=%wide.region_3.4_spmd.clone.clone, body=%wide.region_2.3_spmd.clone.clone.sunk | while | flops 414191616 | bytes 5492413 | solution.py:92
  203.0 4.7 %fusion.52 = f32[8,512,1,8,64]{1,4,3,2,0:T(8,128)} fusion(f32[8,512,1,8,64]{1,4,3,2,0:T(8,128)} %get-tuple-element.377, s32[]{:T(128)} %get-tuple-element.376, f32[512,512]{1,0:T(8,128)S(1)} %fusion.51, f32[8,512]{1,0:T(8,128)S(1)} %dynamic-slice_bitcast_fusion.2, pred[512,512]{1,0:T(8,128)(4,1)S(1)} %iota_compare_fusion.2, ...), kind=kOutput, calls=%fused_computation.12.clone.1 | convolution fusion | flops 278921216 | bytes 2917376 | tf_op jit(solution)/shard_map/while/body/eval_jaxpr/ghij,jghp->ighp/dot_general | solution.py:81
  210.4 4.6 %fusion.52 = f32[8,512,1,8,64]{1,4,3,2,0:T(8,128)} fusion(f32[8,512,1,8,64]{1,4,3,2,0:T(8,128)} %get-tuple-element.377, s32[]{:T(128)} %get-tuple-element.376, f32[512,512]{1,0:T(8,128)S(1)} %fusion.51, f32[8,512]{1,0:T(8,128)S(1)} %dynamic-slice_bitcast_fusion.2, pred[512,512]{1,0:T(8,128)(4,1)S(1)} %iota_compare_fusion.2, ...), kind=kOutput, calls=%fused_computation.12.clone.1 | convolution fusion | flops 278921216 | bytes 2917376 | tf_op jit(solution)/shard_map/while/body/eval_jaxpr/ghij,jghp->ighp/dot_general | solution.py:81
  217.7 4.7 %fusion.52 = f32[8,512,1,8,64]{1,4,3,2,0:T(8,128)} fusion(f32[8,512,1,8,64]{1,4,3,2,0:T(8,128)} %get-tuple-element.377, s32[]{:T(128)} %get-tuple-element.376, f32[512,512]{1,0:T(8,128)S(1)} %fusion.51, f32[8,512]{1,0:T(8,128)S(1)} %dynamic-slice_bitcast_fusion.2, pred[512,512]{1,0:T(8,128)(4,1)S(1)} %iota_compare_fusion.2, ...), kind=kOutput, calls=%fused_computation.12.clone.1 | convolution fusion | flops 278921216 | bytes 2917376 | tf_op jit(solution)/shard_map/while/body/eval_jaxpr/ghij,jghp->ighp/dot_general | solution.py:81
  225.1 4.7 %fusion.52 = f32[8,512,1,8,64]{1,4,3,2,0:T(8,128)} fusion(f32[8,512,1,8,64]{1,4,3,2,0:T(8,128)} %get-tuple-element.377, s32[]{:T(128)} %get-tuple-element.376, f32[512,512]{1,0:T(8,128)S(1)} %fusion.51, f32[8,512]{1,0:T(8,128)S(1)} %dynamic-slice_bitcast_fusion.2, pred[512,512]{1,0:T(8,128)(4,1)S(1)} %iota_compare_fusion.2, ...), kind=kOutput, calls=%fused_computation.12.clone.1 | convolution fusion | flops 278921216 | bytes 2917376 | tf_op jit(solution)/shard_map/while/body/eval_jaxpr/ghij,jghp->ighp/dot_general | solution.py:81
  232.5 4.7 %fusion.52 = f32[8,512,1,8,64]{1,4,3,2,0:T(8,128)} fusion(f32[8,512,1,8,64]{1,4,3,2,0:T(8,128)} %get-tuple-element.377, s32[]{:T(128)} %get-tuple-element.376, f32[512,512]{1,0:T(8,128)S(1)} %fusion.51, f32[8,512]{1,0:T(8,128)S(1)} %dynamic-slice_bitcast_fusion.2, pred[512,512]{1,0:T(8,128)(4,1)S(1)} %iota_compare_fusion.2, ...), kind=kOutput, calls=%fused_computation.12.clone.1 | convolution fusion | flops 278921216 | bytes 2917376 | tf_op jit(solution)/shard_map/while/body/eval_jaxpr/ghij,jghp->ighp/dot_general | solution.py:81
  239.9 4.6 %fusion.52 = f32[8,512,1,8,64]{1,4,3,2,0:T(8,128)} fusion(f32[8,512,1,8,64]{1,4,3,2,0:T(8,128)} %get-tuple-element.377, s32[]{:T(128)} %get-tuple-element.376, f32[512,512]{1,0:T(8,128)S(1)} %fusion.51, f32[8,512]{1,0:T(8,128)S(1)} %dynamic-slice_bitcast_fusion.2, pred[512,512]{1,0:T(8,128)(4,1)S(1)} %iota_compare_fusion.2, ...), kind=kOutput, calls=%fused_computation.12.clone.1 | convolution fusion | flops 278921216 | bytes 2917376 | tf_op jit(solution)/shard_map/while/body/eval_jaxpr/ghij,jghp->ighp/dot_general | solution.py:81
  247.2 4.7 %fusion.52 = f32[8,512,1,8,64]{1,4,3,2,0:T(8,128)} fusion(f32[8,512,1,8,64]{1,4,3,2,0:T(8,128)} %get-tuple-element.377, s32[]{:T(128)} %get-tuple-element.376, f32[512,512]{1,0:T(8,128)S(1)} %fusion.51, f32[8,512]{1,0:T(8,128)S(1)} %dynamic-slice_bitcast_fusion.2, pred[512,512]{1,0:T(8,128)(4,1)S(1)} %iota_compare_fusion.2, ...), kind=kOutput, calls=%fused_computation.12.clone.1 | convolution fusion | flops 278921216 | bytes 2917376 | tf_op jit(solution)/shard_map/while/body/eval_jaxpr/ghij,jghp->ighp/dot_general | solution.py:81
  254.7 4.6 %fusion.52 = f32[8,512,1,8,64]{1,4,3,2,0:T(8,128)} fusion(f32[8,512,1,8,64]{1,4,3,2,0:T(8,128)} %get-tuple-element.377, s32[]{:T(128)} %get-tuple-element.376, f32[512,512]{1,0:T(8,128)S(1)} %fusion.51, f32[8,512]{1,0:T(8,128)S(1)} %dynamic-slice_bitcast_fusion.2, pred[512,512]{1,0:T(8,128)(4,1)S(1)} %iota_compare_fusion.2, ...), kind=kOutput, calls=%fused_computation.12.clone.1 | convolution fusion | flops 278921216 | bytes 2917376 | tf_op jit(solution)/shard_map/while/body/eval_jaxpr/ghij,jghp->ighp/dot_general | solution.py:81
  261.9 8.9 %while.41 = (s32[]{:T(128)}, f32[8,64,128]{2,1,0:T(8,128)S(1)}, f32[8,8,64,128]{3,2,1,0:T(8,128)S(1)}, f32[8,8]{1,0:T(8,128)S(1)}, f32[8,8,64,128]{3,2,1,0:T(8,128)}, /*index=5*/s32[]{:T(128)}, s32[]{:T(128)}) while((s32[]{:T(128)}, f32[8,64,128]{2,1,0:T(8,128)S(1)}, f32[8,8,64,128]{3,2,1,0:T(8,128)S(1)}, f32[8,8]{1,0:T(8,128)S(1)}, ...), condition=%wide.region_5.6_spmd.clone, body=%wide.region_4.5_spmd.clone.sunk | while | flops 262147 | bytes 1310916 | solution.py:101
  273.2 23.8 %all-reduce = bf16[128]{0:T(256)(128)(2,1)S(1)} all-reduce(bf16[128]{0:T(256)(128)(2,1)S(1)} %dynamic-update-slice), channel_id=2, replica_groups=mesh['seq'=16,'head'=16] {'seq'}, use_global_device_ids=true, to_apply=%add | all-reduce | flops 128 | bytes 512
  297.1 12.5 %all-gather.10.cloned.1.call-done = bf16[128,64,128]{2,1,0:T(8,128)(2,1)} async-done(((bf16[8,64,128]{2,1,0:T(8,128)(2,1)}), bf16[128,64,128]{2,1,0:T(8,128)(2,1)}) %all-gather.10.cloned.1.call-update) | async-done | bytes 2097168 | tf_op jit(solution)/shard_map/all_gather | solution.py:15
  309.6 16.0 %while.39 = (s32[]{:T(128)}, f32[8,64,128]{2,1,0:T(8,128)S(1)}, s32[]{:T(128)}, bf16[16,8]{1,0:T(8,128)(2,1)S(1)}, bf16[16,8,64,128]{3,2,1,0:T(8,128)(2,1)}, /*index=5*/s32[]{:T(128)}, s32[]{:T(128)}, s32[]{:T(128)}) while((s32[]{:T(128)}, f32[8,64,128]{2,1,0:T(8,128)S(1)}, s32[]{:T(128)}, bf16[16,8]{1,0:T(8,128)(2,1)S(1)}, ...), condition=%wide.region_9.10_spmd, body=%wide.region_8.9_spmd.sunk | while | flops 196621 | bytes 655567 | solution.py:29
  325.6 10.9 %fusion.29 = bf16[8,512,1,8,64]{1,4,3,0,2:T(8,128)(2,1)S(1)} fusion(f32[8,512,1,8,64]{1,4,3,2,0:T(8,128)} %get-tuple-element.123, f32[8,512,1,8,64]{1,0,4,3,2:T(8,128)} %reshape.178, f32[8]{0:T(128)S(1)} %dynamic_slice.44, f32[8,512,8]{1,2,0:T(8,128)S(1)} %get-tuple-element.260, bf16[8,512,128,1]{2,1,3,0:T(8,128)(2,1)S(1)} %bitcast.137, ...), kind=kOutput, calls=%fused_computation.40 | convolution fusion | flops 548929536 | bytes 24510752 | tf_op jit(solution)/shard_map/cign,cghpn->cighp/dot_general | solution.py:116
  336.5 4.6 %copy.89 = bf16[8,512,1,8,64]{1,0,4,3,2:T(8,128)(2,1)} copy(bf16[8,512,1,8,64]{1,4,3,0,2:T(8,128)(2,1)S(1)} %fusion.29) | data formatting | bytes 8388608 | tf_op jit(solution)/shard_map/convert_element_type | solution.py:123
  341.0 7.1 %all_to_all.50 = bf16[16,256,512]{1,0,2:T(8,128)(2,1)} reshape(bf16[8,512,1,8,64]{1,0,4,3,2:T(8,128)(2,1)} %copy.89) | data formatting | bytes 8388608 | tf_op jit(solution)/shard_map/all_to_all | solution.py:124
  348.1 3.7 copy.90
  351.8 57.4 %all_to_all.58 = bf16[16,256,512]{1,2,0:T(8,128)(2,1)} all-to-all(bf16[16,256,512]{1,2,0:T(8,128)(2,1)S(1)} %copy.90), channel_id=1, replica_groups=mesh['seq'=16,'head'=16] {'head'}, dimensions={0} | all-to-all | bytes 8388608 | tf_op jit(solution)/shard_map/all_to_all | solution.py:124
  409.2 6.3 %copy.91 = bf16[256,8192]{1,0:T(8,128)(2,1)} copy(bf16[256,8192]{0,1:T(8,128)(2,1)} %bitcast.135) | data formatting | bytes 8388608 | tf_op jit(solution)/shard_map/all_to_all | solution.py:124
  (141 shorter events, 58.1 us)
Async XLA Ops:
  6.5 137.8 %all-gather.6.cloned.1.call-start = ((), (), s32[]{:S(2)}) async-start(), calls=%async_computation.4 | async-start | bytes 8912896 | tf_op jit(solution)/shard_map/all_gather | solution.py:51
  7.3 192.4 %all-gather.8.cloned.1.call-start = ((), (), s32[]{:S(2)}) async-start(), calls=%async_computation.5 | async-start | bytes 8912896 | tf_op jit(solution)/shard_map/all_gather | solution.py:50
  9.6 13.3 %all-to-all-start.2 = ((bf16[256,16,8]{0,2,1:T(8,128)(2,1)}), bf16[256,16,8]{0,2,1:T(8,128)(2,1)S(1)}, u32[]{:S(2)}, u32[]{:S(2)}) async-start(bf16[256,16,8]{0,2,1:T(8,128)(2,1)} %bitcast.102), calls=%async_computation.2 | async-start | bytes 131072 | tf_op jit(solution)/shard_map/all_to_all | solution.py:45
  22.9 10.3 %all-to-all-start.1 = ((bf16[256,16,8]{0,2,1:T(8,128)(2,1)}), bf16[256,16,8]{0,2,1:T(8,128)(2,1)S(1)}, u32[]{:S(2)}, u32[]{:S(2)}) async-start(bf16[256,16,8]{0,2,1:T(8,128)(2,1)} %bitcast.103), calls=%async_computation.1 | async-start | bytes 131072 | tf_op jit(solution)/shard_map/all_to_all | solution.py:42
  33.2 81.6 %all-to-all-start = ((bf16[256,16,512]{0,2,1:T(8,128)(2,1)}), bf16[256,16,512]{0,2,1:T(8,128)(2,1)}, u32[]{:S(2)}, u32[]{:S(2)}) async-start(bf16[256,16,512]{0,2,1:T(8,128)(2,1)} %bitcast.134), calls=%async_computation | async-start | bytes 8388608 | tf_op jit(solution)/shard_map/all_to_all | solution.py:40
  39.5 270.1 %all-gather.10.cloned.1.call-start = ((), (), s32[]{:S(2)}) async-start(), calls=%async_computation.6 | async-start | bytes 2228224 | tf_op jit(solution)/shard_map/all_gather | solution.py:15
  261.6 9.9 %copy-start.1 = (u32[256]{0:T(256)S(1)}, u32[256]{0:T(256)}, u32[]{:S(2)}) copy-start(u32[256]{0:T(256)} %constant.87) | copy-start | bytes 3076
  261.6 11.1 %copy-start = (f32[128]{0:T(128)S(1)}, f32[128]{0:T(128)}, u32[]{:S(2)}) copy-start(f32[128]{0:T(128)} %param.17) | copy-start | bytes 1540
Sparse Core Ops, SparseCore 0:
  9.8 115.7 all-gather.5
  128.0 71.6 all-gather.7
  271.6 37.8 all-gather.9
where the time goes:
time: 424 us; the launch traced here: 422 us
  waiting for transfers between devices  138 us (33%)
  blocking collectives  81.1 us (19%)
  matrix products  66.9 us (16%)
  local copies, waits for them, and re-layouts  60.3 us (14%)
  other arithmetic  43.7 us (10%)
  starting transfers between devices  16.6 us (4%)
  between operations  14 us (3%)
    all_to_all x1, waiting for transfers between devices, shards(): lax.all_to_all(features, 'head', split_axis=1, concat_axis=0, tiled=True)  65.2 us
    all_to_all x1, blocking collectives, shards(): lax.all_to_all(mixed_rows, 'head', split_axis=0, concat_axis=1, tiled=True)  57.4 us
    all_gather x1, waiting for transfers between devices, shards(): lax.all_gather(inject, 'head', axis=0, tiled=True)  54.1 us
    dot_general x8, matrix products, span_terms(): jnp.einsum('ghij,jghp->ighp', weights, drive_c, preferred_element_type=jn...  37.3 us
    unnamed x1, blocking collectives  23.8 us
    convert_element_type x2, local copies, waits for them, and re-layouts, shards(): regrouped.reshape(seq_rows, local_heads, HEAD_DIM).astype(jnp.float32)  17.9 us
    all_to_all x3, local copies, waits for them, and re-layouts, shards(): lax.all_to_all(mixed_rows, 'head', split_axis=0, concat_axis=1, tiled=True)  17.1 us
    dot_general x8, matrix products, span_terms(): jnp.einsum('jghp,jgn->ghpn', scaled, inject_c, preferred_element_type=jnp...  16.4 us
  transfers between devices with their start and end apart: 6, of which 5 were waited for; matrix products, arithmetic and copies ran while one was open for 12% of the time, Pallas kernels for 0%

commit v1 on v0

--- a/solution.py
+++ b/solution.py
@@ -7,6 +7,27 @@
 STATE = 128
 GROUPS = 8
 SPAN = 512
+
+
+def collect(shard, axis, dim):
+    peers, place, width = (lax.axis_size(axis), lax.axis_index(axis), shard.shape[dim])
+    ahead = [(i, (i + 1) % peers) for i in range(peers)]
+    left = [(i, (i - 1) % peers) for i in range(peers)]
+    whole = jnp.zeros((*shard.shape[:dim], peers * width, *shard.shape[dim + 1 :]), shard.dtype)
+    whole = lax.dynamic_update_slice_in_dim(whole, shard, place * width, axis=dim)
+    from_left = from_right = shard
+    halfway = peers // 2
+    for hop in range(1, halfway + 1):
+        from_left = lax.ppermute(from_left, axis, ahead)
+        whole = lax.dynamic_update_slice_in_dim(
+            whole, from_left, (place - hop) % peers * width, axis=dim
+        )
+        if hop < peers - halfway:
+            from_right = lax.ppermute(from_right, axis, left)
+            whole = lax.dynamic_update_slice_in_dim(
+                whole, from_right, (place + hop) % peers * width, axis=dim
+            )
+    return whole
 
 
 def entering_2(x, axis, join, neutral):
@@ -47,7 +68,7 @@
         ).astype(log_decay.dtype),
     )
     inject_all, readout_all = (
-        lax.all_gather(inject, "head", axis=0, tiled=True),
+        collect(inject, "head", 0),
         lax.all_gather(readout, "head", axis=0, tiled=True),
     )
     first_col = head_index * local_heads // group_heads * STATE

time: 424 us -> 486 us (1.15)
  starting transfers between devices: 16.6 us -> 50.6 us
  local copies, waits for them, and re-layouts: 60.3 us -> 82.2 us
  blocking collectives: 81.1 us -> 95 us
  waiting for transfers between devices: 138 us -> 130 us
    ppermute x0 -> x15, waiting for transfers between devices: none -> 105 us  [the longest x8 104 us: collect(): from_left = lax.ppermute(from_left, axis, ahead)]
    all_to_all x1, waiting for transfers between devices: 65.2 us -> 0.01 us  [shards(): lax.all_to_all(features, 'head', split_axis=1, concat_axis=0, tiled=True)]
    all_gather x1 -> x0, waiting for transfers between devices: 54.1 us -> none  [shards(): lax.all_gather(inject, 'head', axis=0, tiled=True)]
    ppermute x0 -> x15, starting transfers between devices: none -> 34.8 us  [the longest x7 32 us: collect(): from_right = lax.ppermute(from_right, axis, left)]
    dynamic_update_slice x0 -> x16, local copies, waits for them, and re-layouts: none -> 17.6 us  [the longest x8 8.79 us: collect(): lax.dynamic_update_slice_in_dim(whole, from_left, (place - hop) % peers *...]
    unnamed x1, blocking collectives: 23.8 us -> 37.6 us
    all_gather x1, waiting for transfers between devices: 12.5 us -> 17.5 us  [entering_2(): lax.all_gather(a.astype(kind), axis)]
    unnamed x11 -> x15, local copies, waits for them, and re-layouts: 14.1 us -> 14 us
  transfers between devices with their start and end apart: 6 -> 20, of which waited for: 5 -> 10; matrix products, arithmetic and copies ran while one was open for 12% -> 15% of each run, Pallas kernels for 0% -> 0%
where the time goes in v1:
time: 486 us; the launch traced here: 483 us
  waiting for transfers between devices  130 us (27%)
  blocking collectives  95 us (20%)
  local copies, waits for them, and re-layouts  82.2 us (17%)
  matrix products  67.1 us (14%)
  starting transfers between devices  50.6 us (10%)
  other arithmetic  43.2 us (9%)
  between operations  14.3 us (3%)
    ppermute x8, waiting for transfers between devices, collect(): from_left = lax.ppermute(from_left, axis, ahead)  104 us
    all_to_all x1, blocking collectives, shards(): lax.all_to_all(mixed_rows, 'head', split_axis=0, concat_axis=1, tiled=True)  57.4 us
    unnamed x1, blocking collectives  37.6 us
    dot_general x8, matrix products, span_terms(): jnp.einsum('ghij,jghp->ighp', weights, drive_c, preferred_element_type=jn...  37.3 us
    ppermute x7, starting transfers between devices, collect(): from_right = lax.ppermute(from_right, axis, left)  32 us
    convert_element_type x2, local copies, waits for them, and re-layouts, shards(): regrouped.reshape(seq_rows, local_heads, HEAD_DIM).astype(jnp.float32)  17.9 us
    all_gather x1, waiting for transfers between devices, entering_2(): lax.all_gather(a.astype(kind), axis)  17.5 us
    all_to_all x3, local copies, waits for them, and re-layouts, shards(): lax.all_to_all(mixed_rows, 'head', split_axis=0, concat_axis=1, tiled=True)  17.1 us
  transfers between devices with their start and end apart: 20, of which 10 were waited for; matrix products, arithmetic and copies ran while one was open for 15% of the time, Pallas kernels for 0%

profile of v1, /device:TPU:225, one launch (start us, length us, event | category | flops | bytes accessed | tf_op | source)
XLA Modules:
  0.0 483.2 jit_solution(8764521442297029578)
XLA Ops:
  19.1 6.0 %all-to-all-done.2 = bf16[256,16,8]{0,2,1:T(8,128)(2,1)S(1)} async-done(((bf16[256,16,8]{0,2,1:T(8,128)(2,1)}), bf16[256,16,8]{0,2,1:T(8,128)(2,1)S(1)}, u32[]{:S(2)}, u32[]{:S(2)}) %all-to-all-start.2) | async-done | bytes 65568 | tf_op jit(solution)/shard_map/all_to_all | solution.py:66
  25.1 5.6 %all-to-all-start.1 = ((bf16[256,16,8]{0,2,1:T(8,128)(2,1)}), bf16[256,16,8]{0,2,1:T(8,128)(2,1)S(1)}, u32[]{:S(2)}, u32[]{:S(2)}) async-start(bf16[256,16,8]{0,2,1:T(8,128)(2,1)} %bitcast.103), calls=%async_computation.1 | async-start | bytes 131072 | tf_op jit(solution)/shard_map/all_to_all | solution.py:63
  30.7 6.4 %copy.78 = bf16[256,8192]{0,1:T(8,128)(2,1)} copy(bf16[256,8192]{1,0:T(8,128)(2,1)} %param.12) | data formatting | bytes 8388608 | tf_op args[0]
  37.4 6.6 %all-to-all-start = ((bf16[256,16,512]{0,2,1:T(8,128)(2,1)}), bf16[256,16,512]{0,2,1:T(8,128)(2,1)}, u32[]{:S(2)}, u32[]{:S(2)}) async-start(bf16[256,16,512]{0,2,1:T(8,128)(2,1)} %bitcast.134), calls=%async_computation | async-start | bytes 8388608 | tf_op jit(solution)/shard_map/all_to_all | solution.py:61
  48.9 81.2 %collective-permute-done.2 = bf16[256,1024]{1,0:T(8,128)(2,1)S(1)} collective-permute-done((bf16[256,1024]{1,0:T(8,128)(2,1)S(1)}, bf16[256,1024]{1,0:T(8,128)(2,1)S(1)}, u32[]{:S(2)}, u32[]{:S(2)}) %collective-permute-start.2) | collective-permute-done | bytes 524320 | tf_op jit(solution)/shard_map/ppermute | solution.py:21
  130.5 5.5 %collective-permute-start.5 = (bf16[256,1024]{1,0:T(8,128)(2,1)S(1)}, bf16[256,1024]{1,0:T(8,128)(2,1)}, u32[]{:S(2)}, u32[]{:S(2)}) collective-permute-start(bf16[256,1024]{1,0:T(8,128)(2,1)S(1)} %collective-permute-done.3), channel_id=1, source_target_pairs={{0,15},{1,0},{2,1},{3,2},{4,3},{5,4},{6,5},{7,6},{8,7},{9,8},{10,9... | collective-permute-start | bytes 1572872 | tf_op jit(solution)/shard_map/ppermute | solution.py:26
  136.0 9.3 %collective-permute-done.4 = bf16[256,1024]{1,0:T(8,128)(2,1)S(1)} collective-permute-done((bf16[256,1024]{1,0:T(8,128)(2,1)S(1)}, bf16[256,1024]{1,0:T(8,128)(2,1)S(1)}, u32[]{:S(2)}, u32[]{:S(2)}) %collective-permute-start.4) | collective-permute-done | bytes 524320 | tf_op jit(solution)/shard_map/ppermute | solution.py:21
  145.3 4.8 collective-permute-start.7
  155.2 9.0 %reduce-window.6 = f32[8,8,4,128]{3,1,2,0:T(8,128)S(1)} reduce-window(f32[8,8,4,128]{3,1,2,0:T(8,128)S(1)} %bitcast.139, f32[]{:T(128)} %constant.158.clone.1), window={size=1x1x1x128 pad=0_0x0_0x0_0x127_0}, to_apply=%region_0.1 | reduce-window | flops 4161536 | bytes 262148 | tf_op jit(solution)/shard_map/reduce-window
  164.8 4.8 collective-permute-start.9
  178.2 4.8 collective-permute-start.11
  194.5 4.9 %collective-permute-start.13 = (bf16[256,1024]{1,0:T(8,128)(2,1)S(1)}, bf16[256,1024]{1,0:T(8,128)(2,1)S(1)}, u32[]{:S(2)}, u32[]{:S(2)}) collective-permute-start(bf16[256,1024]{1,0:T(8,128)(2,1)S(1)} %collective-permute-done.11), channel_id=1, source_target_pairs={{0,15},{1,0},{2,1},{3,2},{4,3},{5,4},{6,5},{7,6},{8,7},{9,8},{10,9... | collective-permute-start | bytes 1572872 | tf_op jit(solution)/shard_map/ppermute | solution.py:26
  202.7 5.2 %collective-permute-done.12 = bf16[256,1024]{1,0:T(8,128)(2,1)S(1)} collective-permute-done((bf16[256,1024]{1,0:T(8,128)(2,1)S(1)}, bf16[256,1024]{1,0:T(8,128)(2,1)S(1)}, u32[]{:S(2)}, u32[]{:S(2)}) %collective-permute-start.12) | collective-permute-done | bytes 524320 | tf_op jit(solution)/shard_map/ppermute | solution.py:21
  213.0 8.1 %copy.79 = f32[16,256,512]{1,0,2:T(8,128)} copy(f32[16,256,512]{1,2,0:T(8,128)S(1)} %convert_bitcast_fusion) | data formatting | bytes 16777216 | tf_op jit(solution)/shard_map/convert_element_type | solution.py:80
  221.1 9.8 %reshape.178 = f32[8,512,1,8,64]{1,0,4,3,2:T(8,128)} reshape(f32[16,256,512]{1,0,2:T(8,128)} %copy.79) | data formatting | bytes 16777216 | tf_op jit(solution)/shard_map/convert_element_type | solution.py:80
  244.2 59.2 %while.40 = (s32[]{:T(128)}, f32[8,512,1,8,64]{1,4,3,2,0:T(8,128)}, f32[8,8,64,128]{3,2,1,0:T(8,128)}, bf16[8,512,1,8,64]{1,4,3,2,0:T(8,128)(2,1)}, f32[8,512,8]...) while((s32[]{:T(128)}, f32[8,512,1,8,64]{1,4,3,2,0:T(8,128)}, ...), condition=%wide.region_3.4_spmd.clone.clone, body=%wide.region_2.3_spmd.clone.clone.sunk | while | flops 414191616 | bytes 5492413 | solution.py:113
  244.6 4.7 fusion.52
  252.0 4.7 fusion.52
  259.4 4.7 fusion.52
  266.8 4.6 fusion.52
  274.2 4.7 fusion.52
  281.6 4.7 fusion.52
  289.0 4.7 fusion.52
  296.4 4.7 fusion.52
  303.7 8.9 %while.41 = (s32[]{:T(128)}, f32[8,64,128]{2,1,0:T(8,128)S(1)}, f32[8,8,64,128]{3,2,1,0:T(8,128)S(1)}, f32[8,8]{1,0:T(8,128)S(1)}, f32[8,8,64,128]{3,2,1,0:T(8,128)}, /*index=5*/s32[]{:T(128)}, s32[]{:T(128)}) while((s32[]{:T(128)}, f32[8,64,128]{2,1,0:T(8,128)S(1)}, f32[8,8,64,128]{3,2,1,0:T(8,128)S(1)}, f32[8,8]{1,0:T(8,128)S(1)}, ...), condition=%wide.region_5.6_spmd.clone, body=%wide.region_4.5_spmd.clone.sunk | while | flops 262147 | bytes 1310916 | solution.py:122
  314.9 37.6 %all-reduce = bf16[128]{0:T(256)(128)(2,1)S(1)} all-reduce(bf16[128]{0:T(256)(128)(2,1)S(1)} %dynamic-update-slice), channel_id=2, replica_groups=mesh['seq'=16,'head'=16] {'seq'}, use_global_device_ids=true, to_apply=%add | all-reduce | flops 128 | bytes 512
  352.6 17.5 %all-gather.7.cloned.1.call-done = bf16[128,64,128]{2,1,0:T(8,128)(2,1)} async-done(((bf16[8,64,128]{2,1,0:T(8,128)(2,1)}), bf16[128,64,128]{2,1,0:T(8,128)(2,1)}) %all-gather.7.cloned.1.call-update) | async-done | bytes 2097168 | tf_op jit(solution)/shard_map/all_gather | solution.py:36
  370.1 16.2 %while.39 = (s32[]{:T(128)}, f32[8,64,128]{2,1,0:T(8,128)S(1)}, s32[]{:T(128)}, bf16[16,8]{1,0:T(8,128)(2,1)S(1)}, bf16[16,8,64,128]{3,2,1,0:T(8,128)(2,1)}, /*index=5*/s32[]{:T(128)}, s32[]{:T(128)}, s32[]{:T(128)}) while((s32[]{:T(128)}, f32[8,64,128]{2,1,0:T(8,128)S(1)}, s32[]{:T(128)}, bf16[16,8]{1,0:T(8,128)(2,1)S(1)}, ...), condition=%wide.region_9.10_spmd, body=%wide.region_8.9_spmd.sunk | while | flops 196621 | bytes 655567 | solution.py:50
  386.4 10.9 %fusion.29 = bf16[8,512,1,8,64]{1,4,3,0,2:T(8,128)(2,1)S(1)} fusion(f32[8,512,1,8,64]{1,4,3,2,0:T(8,128)} %get-tuple-element.123, f32[8,512,1,8,64]{1,0,4,3,2:T(8,128)} %reshape.178, f32[8]{0:T(128)S(1)} %dynamic_slice.44, f32[8,512,8]{1,2,0:T(8,128)S(1)} %get-tuple-element.260, bf16[8,512,128,1]{2,1,3,0:T(8,128)(2,1)S(1)} %bitcast.137, ...), kind=kOutput, calls=%fused_computation.40 | convolution fusion | flops 548929536 | bytes 24510752 | tf_op jit(solution)/shard_map/cign,cghpn->cighp/dot_general | solution.py:137
  401.8 7.1 %all_to_all.50 = bf16[16,256,512]{1,0,2:T(8,128)(2,1)} reshape(bf16[8,512,1,8,64]{1,0,4,3,2:T(8,128)(2,1)} %copy.89) | data formatting | bytes 8388608 | tf_op jit(solution)/shard_map/all_to_all | solution.py:145
  412.6 57.4 %all_to_all.58 = bf16[16,256,512]{1,2,0:T(8,128)(2,1)} all-to-all(bf16[16,256,512]{1,2,0:T(8,128)(2,1)S(1)} %copy.90), channel_id=1, replica_groups=mesh['seq'=16,'head'=16] {'head'}, dimensions={0} | all-to-all | bytes 8388608 | tf_op jit(solution)/shard_map/all_to_all | solution.py:145
  470.0 6.3 %copy.91 = bf16[256,8192]{1,0:T(8,128)(2,1)} copy(bf16[256,8192]{0,1:T(8,128)(2,1)} %bitcast.135) | data formatting | bytes 8388608 | tf_op jit(solution)/shard_map/all_to_all | solution.py:145
  (189 shorter events, 121.6 us)
Async XLA Ops:
  6.5 234.7 %all-gather.5.cloned.1.call-start = ((), (), s32[]{:S(2)}) async-start(), calls=%async_computation.4 | async-start | bytes 8912896 | tf_op jit(solution)/shard_map/all_gather | solution.py:72
  7.3 36.7 %collective-permute-start = (bf16[256,1024]{1,0:T(8,128)(2,1)}, bf16[256,1024]{1,0:T(8,128)(2,1)S(1)}, u32[]{:S(2)}, u32[]{:S(2)}) collective-permute-start(bf16[256,1024]{1,0:T(8,128)(2,1)} %param.15), channel_id=1, source_target_pairs={{0,1},{1,2},{2,3},{3,4},{4,5},{5,6},{6,7},{7,8},{8,9},{9,10},{10,1... | collective-permute-start | bytes 1572872 | tf_op jit(solution)/shard_map/ppermute | solution.py:21
  8.6 36.8 %collective-permute-start.1 = (bf16[256,1024]{1,0:T(8,128)(2,1)}, bf16[256,1024]{1,0:T(8,128)(2,1)S(1)}, u32[]{:S(2)}, u32[]{:S(2)}) collective-permute-start(bf16[256,1024]{1,0:T(8,128)(2,1)} %param.15), channel_id=1, source_target_pairs={{0,15},{1,0},{2,1},{3,2},{4,3},{5,4},{6,5},{7,6},{8,7},{9,8},{10,9... | collective-permute-start | bytes 1572872 | tf_op jit(solution)/shard_map/ppermute | solution.py:26
  14.0 11.1 %all-to-all-start.2 = ((bf16[256,16,8]{0,2,1:T(8,128)(2,1)}), bf16[256,16,8]{0,2,1:T(8,128)(2,1)S(1)}, u32[]{:S(2)}, u32[]{:S(2)}) async-start(bf16[256,16,8]{0,2,1:T(8,128)(2,1)} %bitcast.102), calls=%async_computation.2 | async-start | bytes 131072 | tf_op jit(solution)/shard_map/all_to_all | solution.py:66
  25.1 12.3 %all-to-all-start.1 = ((bf16[256,16,8]{0,2,1:T(8,128)(2,1)}), bf16[256,16,8]{0,2,1:T(8,128)(2,1)S(1)}, u32[]{:S(2)}, u32[]{:S(2)}) async-start(bf16[256,16,8]{0,2,1:T(8,128)(2,1)} %bitcast.103), calls=%async_computation.1 | async-start | bytes 131072 | tf_op jit(solution)/shard_map/all_to_all | solution.py:63
  37.4 117.0 %copy-start = (bf16[256,1024]{1,0:T(8,128)(2,1)S(1)}, bf16[256,1024]{1,0:T(8,128)(2,1)}, u32[]{:S(2)}) copy-start(bf16[256,1024]{1,0:T(8,128)(2,1)} %param.15) | copy-start | bytes 1572868
  37.4 172.6 %all-to-all-start = ((bf16[256,16,512]{0,2,1:T(8,128)(2,1)}), bf16[256,16,512]{0,2,1:T(8,128)(2,1)}, u32[]{:S(2)}, u32[]{:S(2)}) async-start(bf16[256,16,512]{0,2,1:T(8,128)(2,1)} %bitcast.134), calls=%async_computation | async-start | bytes 8388608 | tf_op jit(solution)/shard_map/all_to_all | solution.py:61
  44.0 326.1 %all-gather.7.cloned.1.call-start = ((), (), s32[]{:S(2)}) async-start(), calls=%async_computation.5 | async-start | bytes 2228224 | tf_op jit(solution)/shard_map/all_gather | solution.py:36
  44.0 86.1 %collective-permute-start.2 = (bf16[256,1024]{1,0:T(8,128)(2,1)S(1)}, bf16[256,1024]{1,0:T(8,128)(2,1)S(1)}, u32[]{:S(2)}, u32[]{:S(2)}) collective-permute-start(bf16[256,1024]{1,0:T(8,128)(2,1)S(1)} %collective-permute-done), channel_id=1, source_target_pairs={{0,1},{1,2},{2,3},{3,4},{4,5},{5,6},{6,7},{7,8},{8,9},{9,10},{10,1... | collective-permute-start | bytes 1572872 | tf_op jit(solution)/shard_map/ppermute | solution.py:21
  45.4 85.1 %collective-permute-start.3 = (bf16[256,1024]{1,0:T(8,128)(2,1)S(1)}, bf16[256,1024]{1,0:T(8,128)(2,1)S(1)}, u32[]{:S(2)}, u32[]{:S(2)}) collective-permute-start(bf16[256,1024]{1,0:T(8,128)(2,1)S(1)} %collective-permute-done.1), channel_id=1, source_target_pairs={{0,15},{1,0},{2,1},{3,2},{4,3},{5,4},{6,5},{7,6},{8,7},{9,8},{10,9... | collective-permute-start | bytes 1572872 | tf_op jit(solution)/shard_map/ppermute | solution.py:26
  130.1 15.1 %copy-start.1 = (bf16[256,1024]{1,0:T(8,128)(2,1)}, bf16[256,1024]{1,0:T(8,128)(2,1)S(1)}, u32[]{:S(2)}) copy-start(bf16[256,1024]{1,0:T(8,128)(2,1)S(1)} %collective-permute-done.2) | copy-start | bytes 1572868
  130.1 15.1 %collective-permute-start.4 = (bf16[256,1024]{1,0:T(8,128)(2,1)S(1)}, bf16[256,1024]{1,0:T(8,128)(2,1)S(1)}, u32[]{:S(2)}, u32[]{:S(2)}) collective-permute-start(bf16[256,1024]{1,0:T(8,128)(2,1)S(1)} %collective-permute-done.2), channel_id=1, source_target_pairs={{0,1},{1,2},{2,3},{3,4},{4,5},{5,6},{6,7},{7,8},{8,9},{9,10},{10,1... | collective-permute-start | bytes 1572872 | tf_op jit(solution)/shard_map/ppermute | solution.py:21
  130.5 14.8 %collective-permute-start.5 = (bf16[256,1024]{1,0:T(8,128)(2,1)S(1)}, bf16[256,1024]{1,0:T(8,128)(2,1)}, u32[]{:S(2)}, u32[]{:S(2)}) collective-permute-start(bf16[256,1024]{1,0:T(8,128)(2,1)S(1)} %collective-permute-done.3), channel_id=1, source_target_pairs={{0,15},{1,0},{2,1},{3,2},{4,3},{5,4},{6,5},{7,6},{8,7},{9,8},{10,9... | collective-permute-start | bytes 1572872 | tf_op jit(solution)/shard_map/ppermute | solution.py:26
  145.2 19.5 %collective-permute-start.6 = (bf16[256,1024]{1,0:T(8,128)(2,1)S(1)}, bf16[256,1024]{1,0:T(8,128)(2,1)}, u32[]{:S(2)}, u32[]{:S(2)}) collective-permute-start(bf16[256,1024]{1,0:T(8,128)(2,1)S(1)} %collective-permute-done.4), channel_id=1, source_target_pairs={{0,1},{1,2},{2,3},{3,4},{4,5},{5,6},{6,7},{7,8},{8,9},{9,10},{10,1... | collective-permute-start | bytes 1572872 | tf_op jit(solution)/shard_map/ppermute | solution.py:21
  145.3 19.5 %collective-permute-start.7 = (bf16[256,1024]{1,0:T(8,128)(2,1)}, bf16[256,1024]{1,0:T(8,128)(2,1)}, u32[]{:S(2)}, u32[]{:S(2)}) collective-permute-start(bf16[256,1024]{1,0:T(8,128)(2,1)} %collective-permute-done.5), channel_id=1, source_target_pairs={{0,15},{1,0},{2,1},{3,2},{4,3},{5,4},{6,5},{7,6},{8,7},{9,8},{10,9... | collective-permute-start | bytes 1572872 | tf_op jit(solution)/shard_map/ppermute | solution.py:26
  164.7 11.6 %collective-permute-start.8 = (bf16[256,1024]{1,0:T(8,128)(2,1)}, bf16[256,1024]{1,0:T(8,128)(2,1)S(1)}, u32[]{:S(2)}, u32[]{:S(2)}) collective-permute-start(bf16[256,1024]{1,0:T(8,128)(2,1)} %collective-permute-done.6), channel_id=1, source_target_pairs={{0,1},{1,2},{2,3},{3,4},{4,5},{5,6},{6,7},{7,8},{8,9},{9,10},{10,1... | collective-permute-start | bytes 1572872 | tf_op jit(solution)/shard_map/ppermute | solution.py:21
  164.8 13.4 %collective-permute-start.9 = (bf16[256,1024]{1,0:T(8,128)(2,1)}, bf16[256,1024]{1,0:T(8,128)(2,1)S(1)}, u32[]{:S(2)}, u32[]{:S(2)}) collective-permute-start(bf16[256,1024]{1,0:T(8,128)(2,1)} %collective-permute-done.7), channel_id=1, source_target_pairs={{0,15},{1,0},{2,1},{3,2},{4,3},{5,4},{6,5},{7,6},{8,7},{9,8},{10,9... | collective-permute-start | bytes 1572872 | tf_op jit(solution)/shard_map/ppermute | solution.py:26
  176.3 16.2 %collective-permute-start.10 = (bf16[256,1024]{1,0:T(8,128)(2,1)S(1)}, bf16[256,1024]{1,0:T(8,128)(2,1)S(1)}, u32[]{:S(2)}, u32[]{:S(2)}) collective-permute-start(bf16[256,1024]{1,0:T(8,128)(2,1)S(1)} %collective-permute-done.8), channel_id=1, source_target_pairs={{0,1},{1,2},{2,3},{3,4},{4,5},{5,6},{6,7},{7,8},{8,9},{9,10},{10,1... | collective-permute-start | bytes 1572872 | tf_op jit(solution)/shard_map/ppermute | solution.py:21
  178.2 16.3 %collective-permute-start.11 = (bf16[256,1024]{1,0:T(8,128)(2,1)S(1)}, bf16[256,1024]{1,0:T(8,128)(2,1)S(1)}, u32[]{:S(2)}, u32[]{:S(2)}) collective-permute-start(bf16[256,1024]{1,0:T(8,128)(2,1)S(1)} %collective-permute-done.9), channel_id=1, source_target_pairs={{0,15},{1,0},{2,1},{3,2},{4,3},{5,4},{6,5},{7,6},{8,7},{9,8},{10,9... | collective-permute-start | bytes 1572872 | tf_op jit(solution)/shard_map/ppermute | solution.py:26
  192.6 15.3 %collective-permute-start.12 = (bf16[256,1024]{1,0:T(8,128)(2,1)S(1)}, bf16[256,1024]{1,0:T(8,128)(2,1)S(1)}, u32[]{:S(2)}, u32[]{:S(2)}) collective-permute-start(bf16[256,1024]{1,0:T(8,128)(2,1)S(1)} %collective-permute-done.10), channel_id=1, source_target_pairs={{0,1},{1,2},{2,3},{3,4},{4,5},{5,6},{6,7},{7,8},{8,9},{9,10},{10,1... | collective-permute-start | bytes 1572872 | tf_op jit(solution)/shard_map/ppermute | solution.py:21
  194.5 14.6 %collective-permute-start.13 = (bf16[256,1024]{1,0:T(8,128)(2,1)S(1)}, bf16[256,1024]{1,0:T(8,128)(2,1)S(1)}, u32[]{:S(2)}, u32[]{:S(2)}) collective-permute-start(bf16[256,1024]{1,0:T(8,128)(2,1)S(1)} %collective-permute-done.11), channel_id=1, source_target_pairs={{0,15},{1,0},{2,1},{3,2},{4,3},{5,4},{6,5},{7,6},{8,7},{9,8},{10,9... | collective-permute-start | bytes 1572872 | tf_op jit(solution)/shard_map/ppermute | solution.py:26
  207.9 31.2 %collective-permute-start.14 = (bf16[256,1024]{1,0:T(8,128)(2,1)S(1)}, bf16[256,1024]{1,0:T(8,128)(2,1)S(1)}, u32[]{:S(2)}, u32[]{:S(2)}) collective-permute-start(bf16[256,1024]{1,0:T(8,128)(2,1)S(1)} %collective-permute-done.12), channel_id=1, source_target_pairs={{0,1},{1,2},{2,3},{3,4},{4,5},{5,6},{6,7},{7,8},{8,9},{9,10},{10,1... | collective-permute-start | bytes 1572872 | tf_op jit(solution)/shard_map/ppermute | solution.py:21
  303.4 9.9 %copy-start.3 = (u32[256]{0:T(256)S(1)}, u32[256]{0:T(256)}, u32[]{:S(2)}) copy-start(u32[256]{0:T(256)} %constant.186) | copy-start | bytes 3076
  303.4 11.2 %copy-start.2 = (f32[128]{0:T(128)S(1)}, f32[128]{0:T(128)}, u32[]{:S(2)}) copy-start(f32[128]{0:T(128)} %param.17) | copy-start | bytes 1540
Sparse Core Ops, SparseCore 0:
  9.8 133.6 all-gather.4
  313.4 56.6 all-gather.6
